TPU v7x, 256 devices: a whole 4x4x8 slice. The times are simulated.
256 devices in a mesh: wide: 64 (over y, z, core), narrow: 4 (over x).
Axes of the slice: x: 4, y: 4, z: 8, core: 2. Of those that a mesh axis runs over, the one named last changes fastest.
Arguments:
- patches: bfloat16 [65536, 1280], P('wide', 'narrow'), may hold values from -6 to 6
- norm_gain: float32 [1280], replicated, may hold values from 0.1 to 1.9
- norm_bias: float32 [1280], replicated, may hold values from -3 to 3
- w_in: bfloat16 [1280, 5120], P('wide', 'narrow'), may hold values from -0.15625 to 0.15625
- b_in: float32 [5120], P('narrow'), may hold values from -3 to 3
- w_out: bfloat16 [5120, 1280], P('narrow', 'wide'), may hold values from -0.078125 to 0.078125
- b_out: float32 [1280], P('narrow'), may hold values from -3 to 3
- w_proj: bfloat16 [4, 1280, 1280], P(None, 'narrow', 'wide'), may hold values from -0.078125 to 0.078125
- b_proj: float32 [1280], P('narrow'), may hold values from -3 to 3
- text: bfloat16 [32768, 1280], P('wide', 'narrow'), may hold values from -6 to 6
- place: int32 [16384], replicated, may hold values from -1 to 32767, as said below
Outputs:
- prompt_embeds: bfloat16 [32768, 1280], P('wide', 'narrow')
Inputs may be any that keep to these rules, and one draw needn't show every extreme that they name: `place`: of the 256 entries of one wide index (entries i * 256 to (i + 1) * 256 - 1), the valid ones (>= 0) come first and -1 fills the rest; three quarters or more are valid, and all are valid for some wide index. Valid values are distinct. For one wide index, at most 8 valid entries v have the same v // 512, and every wide index reaches 8 for some value.
All inputs are finite; a program needn't handle non-finite values.
Results may differ from a plain program's by a relative error of at most 0.012.
Values may be sent and summed in bfloat16 or wider, within the bound.
A program may use at most 64 MiB of HBM per device.

v0:
```python
import jax
import jax.numpy as jnp
from jax import lax
from jax.sharding import PartitionSpec as P


def select_rows(index, rows, count):
    pick = (jnp.arange(count, dtype=jnp.int32)[:, None] == index[None, :]).astype(rows.dtype)
    return jnp.dot(pick, rows, preferred_element_type=jnp.float32).astype(rows.dtype)


def per_device(
    patches, norm_gain, norm_bias, w_in, b_in, w_out, b_out, w_proj, b_proj, text, place
):
    groups = lax.axis_size("wide")
    width = w_in.shape[0]
    local = jnp.concatenate([w_in, w_out.T, w_proj.transpose(2, 0, 1).reshape(width, -1)], axis=0)
    gathered = lax.all_gather(local, "wide", axis=0, tiled=False)
    rows_in = gathered[:, :width].reshape(groups * width, -1)
    cols_out = gathered[:, width : 2 * width].reshape(groups * width, -1)
    proj_cols = gathered[:, 2 * width :].reshape(groups * width, -1)
    whole = lax.all_gather(patches, "narrow", axis=1, tiled=True)
    values = whole.astype(jnp.float32)
    center = jnp.mean(values, axis=-1, keepdims=True)
    spread = jnp.mean(jnp.square(values - center), axis=-1, keepdims=True)
    normed = ((values - center) * lax.rsqrt(spread + 1e-06) * norm_gain + norm_bias).astype(
        jnp.bfloat16
    )
    product = jnp.dot(normed, rows_in, preferred_element_type=jnp.float32)
    hidden = jax.nn.gelu(product + b_in, approximate=False).astype(jnp.bfloat16)
    partial_out = lax.dot_general(
        hidden, cols_out, (((1,), (1,)), ((), ())), preferred_element_type=jnp.float32
    )
    mlp_out = lax.psum_scatter(
        partial_out.astype(jnp.bfloat16), "narrow", scatter_dimension=1, tiled=True
    ).astype(jnp.float32)
    stream = (patches.astype(jnp.float32) + (mlp_out + b_out)).astype(jnp.bfloat16)
    merge_count = stream.shape[0] // 4
    merged = stream.reshape(merge_count, 4 * stream.shape[1])
    own_index = lax.axis_index("wide")
    seq_rows = text.shape[0]
    bucket = seq_rows // groups
    place_table = place.reshape(groups, merge_count)
    owners = jnp.where(place_table >= 0, place_table // seq_rows, groups)
    own_owners = lax.dynamic_index_in_dim(owners, own_index, 0, keepdims=False)
    owner_hits = (own_owners[:, None] == jnp.arange(groups, dtype=jnp.int32)[None, :]).astype(
        jnp.int32
    )
    slot_out = jnp.sum(jnp.cumsum(owner_hits, axis=0) * owner_hits, axis=1) - 1
    send_row = jnp.where(
        (own_owners < groups) & (slot_out < bucket), own_owners * bucket + slot_out, -1
    )
    arriving = owners == own_index
    slot_in = jnp.cumsum(arriving.astype(jnp.int32), axis=1) - 1
    slot_in = jnp.where(arriving, slot_in, bucket)
    local_row = place_table % seq_rows
    slot_hits = slot_in[:, :, None] == jnp.arange(bucket, dtype=jnp.int32)[None, None, :]
    targets = jnp.sum(jnp.where(slot_hits, local_row[:, :, None] + 1, 0), axis=1) - 1
    partial_proj = lax.dot_general(
        merged, proj_cols, (((1,), (1,)), ((), ())), preferred_element_type=jnp.float32
    )
    vision = (
        lax.psum_scatter(
            partial_proj.astype(jnp.bfloat16), "narrow", scatter_dimension=1, tiled=True
        ).astype(jnp.float32)
        + b_proj
    ).astype(jnp.bfloat16)
    outgoing = select_rows(send_row, vision, groups * bucket).reshape(groups, bucket, -1)
    received = lax.all_to_all(outgoing, "wide", split_axis=0, concat_axis=0, tiled=True)
    flat_targets = targets.reshape(-1)
    placed = select_rows(flat_targets, received.reshape(-1, received.shape[2]), seq_rows)
    hit = jnp.any(jnp.arange(seq_rows, dtype=jnp.int32)[:, None] == flat_targets[None, :], axis=1)
    return jnp.where(hit[:, None], placed, text)


def solution(mesh):
    placed = (
        P("wide", "narrow"),
        P(),
        P(),
        P("wide", "narrow"),
        P("narrow"),
        P("narrow", "wide"),
        P("narrow"),
        P(None, "narrow", "wide"),
        P("narrow"),
        P("wide", "narrow"),
        P(),
    )
    return jax.shard_map(
        per_device, mesh=mesh, in_specs=placed, out_specs=P("wide", "narrow"), check_vma=False
    )
```

profile of v0, /device:TPU:1, one launch (start us, length us, event | category | flops | bytes accessed | tf_op | source)
XLA Modules:
  0.0 286.6 jit_solution(14069685264983872683)
XLA Ops:
  6.5 0.0 all-gather.5.cloned.1.call-start
  6.5 0.7 all-gather.5.cloned.1.call-update
  7.3 0.0 all-gather.7.cloned.1.call-start
  7.3 0.9 reshape.177
  8.2 1.6 maximum_bitcast_fusion
  9.8 0.0 all-gather.7.cloned.1.call-update
  9.8 0.0 reduce-scatter.5.cloned.1.call-start
  9.9 40.8 %all-gather.5.cloned.1.call-done = bf16[1024,1280]{0,1:T(8,128)(2,1)} async-done(((bf16[1024,320]{0,1:T(8,128)(2,1)}), bf16[1024,1280]{0,1:T(8,128)(2,1)}) %all-gather.5.cloned.1.call-update) | async-done | bytes 2621456 | tf_op jit(solution)/shard_map/all_gather | solution.py:22
  50.7 2.2 convert_reduce_fusion
  52.9 2.5 fusion.2
  55.4 85.1 %all-gather.7.cloned.1.call-done = bf16[64,60,1280]{2,1,0:T(8,128)(2,1)} async-done(((bf16[1,60,1280]{2,1,0:T(8,128)(2,1)}), bf16[64,60,1280]{2,1,0:T(8,128)(2,1)}) %all-gather.7.cloned.1.call-update) | async-done | bytes 9830416 | tf_op jit(solution)/shard_map/all_gather | solution.py:18
  140.5 8.2 %fusion.72 = (bf16[64,20,1280]{2,1,0:T(8,128)(2,1)}, bf16[64,20,1280]{2,1,0:T(8,128)(2,1)}, bf16[64,20,1280]{2,1,0:T(8,128)(2,1)}) fusion(bf16[64,60,1280]{2,1,0:T(8,128)(2,1)} %all-gather.7.cloned.1.call-done), kind=kLoop, calls=%fused_computation.116 | loop fusion | bytes 19660800 | tf_op jit(solution)/shard_map/slice | solution.py:21
  148.7 6.1 %reshape.179 = bf16[1280,1280]{1,0:T(8,128)(2,1)} reshape(bf16[64,20,1280]{2,1,0:T(8,128)(2,1)} %get-tuple-element.6) | data formatting | bytes 6553600 | tf_op jit(solution)/shard_map/reshape | solution.py:20
  154.9 6.3 %reshape.178 = bf16[1280,1280]{1,0:T(8,128)(2,1)} reshape(bf16[64,20,1280]{2,1,0:T(8,128)(2,1)} %get-tuple-element.7) | data formatting | bytes 6553600 | tf_op jit(solution)/shard_map/reshape | solution.py:19
  161.2 0.0 copy-done
  161.2 0.0 copy-done.3
  161.2 0.0 copy-done.4
  161.2 0.0 copy-done.5
  161.2 0.0 copy-start.1
  161.2 21.5 %convolution_convert_fusion = bf16[1024,1280]{0,1:T(8,128)(2,1)} fusion(bf16[1280,1280]{1,0:T(8,128)(2,1)} %reshape.179, bf16[1280,1280]{1,0:T(8,128)(2,1)} %reshape.178, bf16[1024,1280]{0,1:T(8,128)(2,1)S(1)} %copy-done, f32[1280]{0:T(1024)S(1)} %copy-done.3, f32[1280]{0:T(1024)S(1)} %copy-done.4, f32[1280]{0:T(1024)S(1)} %copy-done.5, ...), kind=kOutput, calls=%fused_computation.27 | convolution fusion | flops 6806568960 | bytes 11820032 | tf_op jit(solution)/shard_map/dot_general | solution.py:31
  182.7 0.0 reduce-scatter.5.cloned.1.call-update
  182.7 0.0 reduce-scatter.7.cloned.1.call-start
  182.8 0.0 copy-done.1
  182.8 0.1 fusion.40
  182.9 0.6 reduce-window.14
  183.5 4.6 %reshape.181 = bf16[1280,1280]{1,0:T(8,128)(2,1)S(1)} reshape(bf16[64,20,1280]{2,1,0:T(8,128)(2,1)} %get-tuple-element.5) | data formatting | bytes 6553600 | tf_op jit(solution)/shard_map/reshape | solution.py:21
  188.1 27.8 %reduce-scatter.5.cloned.1.call-done = bf16[1024,320]{0,1:T(8,128)(2,1)} async-done(((bf16[1024,1280]{0,1:T(8,128)(2,1)}), bf16[1024,320]{0,1:T(8,128)(2,1)}) %reduce-scatter.5.cloned.1.call-update) | async-done | bytes 655376 | tf_op jit(solution)/shard_map/reduce_scatter | solution.py:34
  215.9 0.0 copy-done.2
  215.9 2.4 add_convert_fusion
  218.3 2.2 copy.38
  220.5 2.5 reshape.180
  223.0 3.0 %fusion.21 = bf16[1280,256]{1,0:T(8,128)(2,1)} fusion(bf16[256,1280]{1,0:T(8,128)(2,1)} %reshape.180, bf16[1280,1280]{1,0:T(8,128)(2,1)S(1)} %reshape.181), kind=kOutput, calls=%fused_computation.33 | convolution fusion | flops 839188480 | bytes 4587520 | tf_op jit(solution)/shard_map/dot_general | solution.py:59
  226.0 0.0 reduce-scatter.7.cloned.1.call-update
  226.0 0.2 slice_reduce_fusion.1
  226.3 0.1 fusion.30
  226.4 0.6 reduce-window.16
  227.0 0.2 slice_reduce_fusion
  227.2 0.1 fusion.36
  227.4 21.8 %reduce-scatter.7.cloned.1.call-done = bf16[320,256]{1,0:T(8,128)(2,1)} async-done(((bf16[1280,256]{1,0:T(8,128)(2,1)}), bf16[320,256]{1,0:T(8,128)(2,1)}) %reduce-scatter.7.cloned.1.call-update) | async-done | bytes 163856
  249.1 1.1 copy.42
  250.2 0.3 convolution_convert_fusion.2
  250.6 0.9 copy.40
  251.5 11.8 %all-to-all-start = ((bf16[64,8,320]{2,1,0:T(8,128)(2,1)}), bf16[64,8,320]{2,1,0:T(8,128)(2,1)S(1)}, u32[]{:S(2)}, u32[]{:S(2)}) async-start(bf16[64,8,320]{2,1,0:T(8,128)(2,1)} %bitcast.9), calls=%async_computation.1 | async-start | bytes 786432 | tf_op jit(solution)/shard_map/all_to_all | solution.py:69
  263.3 1.2 select_reduce_fusion
  264.5 0.1 sub.43
  264.6 0.2 fusion.25
  264.8 13.2 %all-to-all-done = bf16[64,8,320]{2,1,0:T(8,128)(2,1)S(1)} async-done(((bf16[64,8,320]{2,1,0:T(8,128)(2,1)}), bf16[64,8,320]{2,1,0:T(8,128)(2,1)S(1)}, u32[]{:S(2)}, u32[]{:S(2)}) %all-to-all-start) | async-done | bytes 327712 | tf_op jit(solution)/shard_map/all_to_all | solution.py:69
  277.9 2.1 fusion.24
  (19 shorter events, 0.2 us)
Async XLA Ops:
  6.5 44.2 %all-gather.5.cloned.1.call-start = ((), (), s32[]{:S(2)}) async-start(), calls=%async_computation.3 | async-start | bytes 3276800 | tf_op jit(solution)/shard_map/all_gather | solution.py:22
  7.3 133.2 %all-gather.7.cloned.1.call-start = ((), (), s32[]{:S(2)}) async-start(), calls=%async_computation.5 | async-start | bytes 10649600 | tf_op jit(solution)/shard_map/all_gather | solution.py:18
  9.8 206.1 %reduce-scatter.5.cloned.1.call-start = ((), (), s32[]{:S(2)}) async-start(), calls=%async_computation.4 | async-start | bytes 3276800 | tf_op jit(solution)/shard_map/reduce_scatter | solution.py:34
  154.9 6.3 %copy-start = (bf16[1024,1280]{0,1:T(8,128)(2,1)S(1)}, bf16[1024,1280]{0,1:T(8,128)(2,1)}, u32[]{:S(2)}) copy-start(bf16[1024,1280]{0,1:T(8,128)(2,1)} %all-gather.5.cloned.1.call-done) | copy-start | bytes 7864324
  154.9 6.3 %copy-start.3 = (f32[1280]{0:T(1024)S(1)}, f32[1280]{0:T(1024)}, u32[]{:S(2)}) copy-start(f32[1280]{0:T(1024)} %param.15) | copy-start | bytes 15364
  154.9 6.3 %copy-start.4 = (f32[1280]{0:T(1024)S(1)}, f32[1280]{0:T(1024)}, u32[]{:S(2)}) copy-start(f32[1280]{0:T(1024)} %param.13) | copy-start | bytes 15364
  154.9 6.3 %copy-start.5 = (f32[1280]{0:T(1024)S(1)}, f32[1280]{0:T(1024)}, u32[]{:S(2)}) copy-start(f32[1280]{0:T(1024)} %param.12) | copy-start | bytes 15364
  161.2 21.6 %copy-start.1 = (s32[16384]{0:T(1024)S(1)}, s32[16384]{0:T(1024)}, u32[]{:S(2)}) copy-start(s32[16384]{0:T(1024)} %param.21) | copy-start | bytes 196612
  182.7 33.2 %copy-start.2 = (f32[320]{0:T(512)S(1)}, f32[320]{0:T(512)}, u32[]{:S(2)}) copy-start(f32[320]{0:T(512)} %param.17) | copy-start | bytes 3844
  182.7 66.4 %reduce-scatter.7.cloned.1.call-start = ((), (), s32[]{:S(2)}) async-start(), calls=%async_computation.6 | async-start | bytes 819200
  218.3 31.9 %copy-start.6 = (f32[320]{0:T(512)S(1)}, f32[320]{0:T(512)}, u32[]{:S(2)}) copy-start(f32[320]{0:T(512)} %param.19) | copy-start | bytes 3844
  251.5 26.4 %all-to-all-start = ((bf16[64,8,320]{2,1,0:T(8,128)(2,1)}), bf16[64,8,320]{2,1,0:T(8,128)(2,1)S(1)}, u32[]{:S(2)}, u32[]{:S(2)}) async-start(bf16[64,8,320]{2,1,0:T(8,128)(2,1)} %bitcast.9), calls=%async_computation.1 | async-start | bytes 786432 | tf_op jit(solution)/shard_map/all_to_all | solution.py:69
Sparse Core Ops, SparseCore 0:
  9.2 41.5 all-gather.4
  53.5 86.9 all-gather.6
  182.8 33.0 reduce-scatter.4
  226.2 22.9 reduce-scatter.6
where the time goes:
time: 287 us
  waiting for transfers between devices  189 us (66%)
  local copies, waits for them, and re-layouts  33.5 us (12%)
  matrix products  26.9 us (9%)
  between operations  13.3 us (5%)
  starting transfers between devices  12 us (4%)
  other arithmetic  11.6 us (4%)
    all_gather x1, waiting for transfers between devices, per_device(): gathered = lax.all_gather(local, 'wide', axis=0, tiled=False)  85.1 us
    all_gather x1, waiting for transfers between devices, per_device(): whole = lax.all_gather(patches, 'narrow', axis=1, tiled=True)  40.8 us
    reduce_scatter x1, waiting for transfers between devices, per_device(): lax.psum_scatter(partial_out.astype(jnp.bfloat16), 'narrow', scatter_dime...  27.8 us
    unnamed x5, waiting for transfers between devices  22.5 us
    dot_general x1, matrix products, per_device(): lax.dot_general(hidden, cols_out, (((1,), (1,)), ((), ())), preferred_ele...  21.5 us
    all_to_all x1, waiting for transfers between devices, per_device(): lax.all_to_all(outgoing, 'wide', split_axis=0, concat_axis=0, tiled=True)  13.2 us
    all_to_all x1, starting transfers between devices, per_device(): lax.all_to_all(outgoing, 'wide', split_axis=0, concat_axis=0, tiled=True)  11.8 us
    slice x1, local copies, waits for them, and re-layouts, per_device(): proj_cols = gathered[:, 2 * width:].reshape(groups * width, -1)  8.25 us
  transfers between devices with their start and end apart: 5, of which 5 were waited for; matrix products, arithmetic and copies ran while one was open for 5% of the time, Pallas kernels for 0%

commit v1 on v0

--- a/solution.py
+++ b/solution.py
@@ -19,7 +19,14 @@
     rows_in = gathered[:, :width].reshape(groups * width, -1)
     cols_out = gathered[:, width : 2 * width].reshape(groups * width, -1)
     proj_cols = gathered[:, 2 * width :].reshape(groups * width, -1)
-    whole = lax.all_gather(patches, "narrow", axis=1, tiled=True)
+    ring = [patches]
+    for hop in range(3):
+        ring.append(lax.ppermute(ring[-1], "narrow", [(dev, (dev + 1) % 4) for dev in range(4)]))
+    whole = jnp.roll(
+        jnp.concatenate(ring[::-1], axis=1),
+        (lax.axis_index("narrow") + 1) * ring[0].shape[1],
+        axis=1,
+    )
     values = whole.astype(jnp.float32)
     center = jnp.mean(values, axis=-1, keepdims=True)
     spread = jnp.mean(jnp.square(values - center), axis=-1, keepdims=True)

time: 287 us -> 243 us (0.85)
  waiting for transfers between devices: 189 us -> 143 us
  starting transfers between devices: 12 us -> 16.8 us
  other arithmetic: 11.6 us -> 7.7 us
    all_gather x1, waiting for transfers between devices: 85.1 us -> 41.5 us  [per_device(): gathered = lax.all_gather(local, 'wide', axis=0, tiled=False)]
    all_gather x1 -> x0, waiting for transfers between devices: 40.8 us -> none  [per_device(): whole = lax.all_gather(patches, 'narrow', axis=1, tiled=True)]
    ppermute x0 -> x3, waiting for transfers between devices: none -> 40.3 us  [per_device(): lax.ppermute(ring[-1], 'narrow', [(dev, (dev + 1) % 4) for dev in range(4)])]
    ppermute x0 -> x3, starting transfers between devices: none -> 4.84 us  [per_device(): lax.ppermute(ring[-1], 'narrow', [(dev, (dev + 1) % 4) for dev in range(4)])]
    unnamed x15 -> x26, local copies, waits for them, and re-layouts: 1.11 us -> 4.08 us
    unnamed x5 -> x4, waiting for transfers between devices: 22.5 us -> 21.7 us
  transfers between devices with their start and end apart: 5 -> 7, of which waited for: 5 -> 7; matrix products, arithmetic and copies ran while one was open for 5% -> 5% of each run, Pallas kernels for 0% -> 0%
where the time goes in v1:
time: 243 us
  waiting for transfers between devices  143 us (59%)
  local copies, waits for them, and re-layouts  34.2 us (14%)
  matrix products  27.6 us (11%)
  starting transfers between devices  16.8 us (7%)
  between operations  13.4 us (6%)
  other arithmetic  7.7 us (3%)
    all_gather x1, waiting for transfers between devices, per_device(): gathered = lax.all_gather(local, 'wide', axis=0, tiled=False)  41.5 us
    ppermute x3, waiting for transfers between devices, per_device(): lax.ppermute(ring[-1], 'narrow', [(dev, (dev + 1) % 4) for dev in range(4)])  40.3 us
    reduce_scatter x1, waiting for transfers between devices, per_device(): lax.psum_scatter(partial_out.astype(jnp.bfloat16), 'narrow', scatter_dime...  26.3 us
    dot_general x1, matrix products, per_device(): lax.dot_general(hidden, cols_out, (((1,), (1,)), ((), ())), preferred_ele...  22.3 us
    unnamed x4, waiting for transfers between devices  21.7 us
    all_to_all x1, waiting for transfers between devices, per_device(): lax.all_to_all(outgoing, 'wide', split_axis=0, concat_axis=0, tiled=True)  13.2 us
    all_to_all x1, starting transfers between devices, per_device(): lax.all_to_all(outgoing, 'wide', split_axis=0, concat_axis=0, tiled=True)  11.9 us
    slice x1, local copies, waits for them, and re-layouts, per_device(): proj_cols = gathered[:, 2 * width:].reshape(groups * width, -1)  8.19 us
  transfers between devices with their start and end apart: 7, of which 7 were waited for; matrix products, arithmetic and copies ran while one was open for 5% of the time, Pallas kernels for 0%

profile of v1, /device:TPU:1, one launch (start us, length us, event | category | flops | bytes accessed | tf_op | source)
XLA Modules:
  0.0 242.7 jit_solution(12030579067904403789)
XLA Ops:
  6.5 1.0 reshape.177
  7.5 1.6 maximum_bitcast_fusion
  9.1 0.0 all-gather.4.cloned.1.call-update
  9.1 0.0 reduce-scatter.5.cloned.1.call-start
  9.2 2.1 collective-permute-start
  11.3 13.6 %collective-permute-done = bf16[1024,320]{0,1:T(8,128)(2,1)S(1)} collective-permute-done((bf16[1024,320]{0,1:T(8,128)(2,1)}, bf16[1024,320]{0,1:T(8,128)(2,1)S(1)}, u32[]{:S(2)}, u32[]{:S(2)}) %collective-permute-start) | collective-permute-done | bytes 655392 | tf_op jit(solution)/shard_map/ppermute | solution.py:24
  24.9 1.9 collective-permute-start.1
  26.8 13.7 %collective-permute-done.1 = bf16[1024,320]{0,1:T(8,128)(2,1)S(1)} collective-permute-done((bf16[1024,320]{0,1:T(8,128)(2,1)S(1)}, bf16[1024,320]{0,1:T(8,128)(2,1)S(1)}, u32[]{:S(2)}, u32[]{:S(2)}) %collective-permute-start.1) | collective-permute-done | bytes 655392 | tf_op jit(solution)/shard_map/ppermute | solution.py:24
  40.5 0.8 collective-permute-start.2
  41.3 13.0 %collective-permute-done.2 = bf16[1024,320]{0,1:T(8,128)(2,1)S(1)} collective-permute-done((bf16[1024,320]{0,1:T(8,128)(2,1)S(1)}, bf16[1024,320]{0,1:T(8,128)(2,1)S(1)}, u32[]{:S(2)}, u32[]{:S(2)}) %collective-permute-start.2) | collective-permute-done | bytes 655392 | tf_op jit(solution)/shard_map/ppermute | solution.py:24
  54.5 1.1 constant_dynamic-update-slice_fusion.4
  55.9 0.8 convert_reduce_fusion
  56.7 1.6 copy-done
  58.2 1.1 fusion.2
  59.3 41.5 %all-gather.4.cloned.1.call-done = bf16[64,60,1280]{2,1,0:T(8,128)(2,1)} async-done(((bf16[1,60,1280]{2,1,0:T(8,128)(2,1)}), bf16[64,60,1280]{2,1,0:T(8,128)(2,1)}) %all-gather.4.cloned.1.call-update) | async-done | bytes 9830416 | tf_op jit(solution)/shard_map/all_gather | solution.py:18
  100.8 8.2 %fusion.76 = (bf16[64,20,1280]{2,1,0:T(8,128)(2,1)}, bf16[64,20,1280]{2,1,0:T(8,128)(2,1)}, bf16[64,20,1280]{2,1,0:T(8,128)(2,1)}) fusion(bf16[64,60,1280]{2,1,0:T(8,128)(2,1)} %all-gather.4.cloned.1.call-done), kind=kLoop, calls=%fused_computation.126 | loop fusion | bytes 19660800 | tf_op jit(solution)/shard_map/slice | solution.py:21
  109.0 6.1 %reshape.179 = bf16[1280,1280]{1,0:T(8,128)(2,1)} reshape(bf16[64,20,1280]{2,1,0:T(8,128)(2,1)} %get-tuple-element.6) | data formatting | bytes 6553600 | tf_op jit(solution)/shard_map/reshape | solution.py:20
  115.1 6.2 %reshape.178 = bf16[1280,1280]{1,0:T(8,128)(2,1)} reshape(bf16[64,20,1280]{2,1,0:T(8,128)(2,1)} %get-tuple-element.7) | data formatting | bytes 6553600 | tf_op jit(solution)/shard_map/reshape | solution.py:19
  121.3 0.0 copy-start.2
  121.3 22.3 %convolution_convert_fusion = bf16[1024,1280]{0,1:T(8,128)(2,1)} fusion(bf16[1280,1280]{1,0:T(8,128)(2,1)} %reshape.179, bf16[1280,1280]{1,0:T(8,128)(2,1)} %reshape.178, f32[1280]{0:T(1024)S(1)} %copy-done.5, f32[1280]{0:T(1024)S(1)} %copy-done.6, f32[1280]{0:T(1024)S(1)} %copy-done.7, f32[1024]{0:T(1024)S(1)} %add_rsqrt_fusion, ...), kind=kOutput, calls=%fused_computation.27 | convolution fusion | flops 6806568960 | bytes 11820036 | tf_op jit(solution)/shard_map/dot_general | solution.py:38
  143.6 0.0 reduce-scatter.5.cloned.1.call-update
  143.6 0.0 reduce-scatter.7.cloned.1.call-start
  143.7 0.1 fusion.42
  143.8 0.6 reduce-window.14
  144.4 6.1 %reshape.181 = bf16[1280,1280]{1,0:T(8,128)(2,1)} reshape(bf16[64,20,1280]{2,1,0:T(8,128)(2,1)} %get-tuple-element.5) | data formatting | bytes 6553600 | tf_op jit(solution)/shard_map/reshape | solution.py:21
  150.5 26.3 %reduce-scatter.5.cloned.1.call-done = bf16[1024,320]{0,1:T(8,128)(2,1)} async-done(((bf16[1024,1280]{0,1:T(8,128)(2,1)}), bf16[1024,320]{0,1:T(8,128)(2,1)}) %reduce-scatter.5.cloned.1.call-update) | async-done | bytes 655376 | tf_op jit(solution)/shard_map/reduce_scatter | solution.py:41
  176.8 1.3 add_convert_fusion
  178.2 0.0 copy-start.8
  178.2 0.4 copy.38
  178.6 0.0 copy-start.4
  178.6 0.7 reshape.180
  179.3 3.8 %fusion.21 = bf16[1280,256]{1,0:T(8,128)(2,1)} fusion(bf16[256,1280]{1,0:T(8,128)(2,1)S(1)} %reshape.180, bf16[1280,1280]{1,0:T(8,128)(2,1)} %reshape.181), kind=kOutput, calls=%fused_computation.33 | convolution fusion | flops 839188480 | bytes 4587520 | tf_op jit(solution)/shard_map/dot_general | solution.py:66
  183.1 0.0 reduce-scatter.7.cloned.1.call-update
  183.1 0.2 slice_reduce_fusion.1
  183.3 0.1 fusion.32
  183.5 0.6 reduce-window.16
  184.1 0.2 slice_reduce_fusion
  184.3 0.1 fusion.38
  184.5 21.7 %reduce-scatter.7.cloned.1.call-done = bf16[320,256]{1,0:T(8,128)(2,1)} async-done(((bf16[1280,256]{1,0:T(8,128)(2,1)}), bf16[320,256]{1,0:T(8,128)(2,1)}) %reduce-scatter.7.cloned.1.call-update) | async-done | bytes 163856
  206.2 1.1 copy.42
  207.3 0.3 convolution_convert_fusion.2
  207.6 0.9 copy.40
  208.5 11.9 %all-to-all-start = ((bf16[64,8,320]{2,1,0:T(8,128)(2,1)}), bf16[64,8,320]{2,1,0:T(8,128)(2,1)S(1)}, u32[]{:S(2)}, u32[]{:S(2)}) async-start(bf16[64,8,320]{2,1,0:T(8,128)(2,1)} %bitcast.9), calls=%async_computation.1 | async-start | bytes 786432 | tf_op jit(solution)/shard_map/all_to_all | solution.py:76
  220.4 1.2 select_reduce_fusion
  221.6 0.1 sub.47
  221.7 0.2 fusion.27
  221.8 13.2 %all-to-all-done = bf16[64,8,320]{2,1,0:T(8,128)(2,1)S(1)} async-done(((bf16[64,8,320]{2,1,0:T(8,128)(2,1)}), bf16[64,8,320]{2,1,0:T(8,128)(2,1)S(1)}, u32[]{:S(2)}, u32[]{:S(2)}) %all-to-all-start) | async-done | bytes 327712 | tf_op jit(solution)/shard_map/all_to_all | solution.py:76
  235.0 1.2 fusion.26
  (34 shorter events, 0.5 us)
Async XLA Ops:
  6.5 49.2 %copy-start.1 = (bf16[1024,320]{0,1:T(8,128)(2,1)S(1)}, bf16[1024,320]{0,1:T(8,128)(2,1)}, u32[]{:S(2)}) copy-start(bf16[1024,320]{0,1:T(8,128)(2,1)} %param.11) | copy-start | bytes 1966084
  6.5 94.3 %all-gather.4.cloned.1.call-start = ((), (), s32[]{:S(2)}) async-start(), calls=%async_computation.4 | async-start | bytes 10649600 | tf_op jit(solution)/shard_map/all_gather | solution.py:18
  9.1 167.7 %reduce-scatter.5.cloned.1.call-start = ((), (), s32[]{:S(2)}) async-start(), calls=%async_computation.3 | async-start | bytes 3276800 | tf_op jit(solution)/shard_map/reduce_scatter | solution.py:41
  9.2 15.8 %collective-permute-start = (bf16[1024,320]{0,1:T(8,128)(2,1)}, bf16[1024,320]{0,1:T(8,128)(2,1)S(1)}, u32[]{:S(2)}, u32[]{:S(2)}) collective-permute-start(bf16[1024,320]{0,1:T(8,128)(2,1)} %param.11), channel_id=1, source_target_pairs={{0,1},{1,2},{2,3},{3,0},{4,5},{5,6},{6,7},{7,4},{8,9},{9,10},{10,1... | collective-permute-start | bytes 1966088 | tf_op jit(solution)/shard_map/ppermute | solution.py:24
  24.9 15.5 %collective-permute-start.1 = (bf16[1024,320]{0,1:T(8,128)(2,1)S(1)}, bf16[1024,320]{0,1:T(8,128)(2,1)S(1)}, u32[]{:S(2)}, u32[]{:S(2)}) collective-permute-start(bf16[1024,320]{0,1:T(8,128)(2,1)S(1)} %collective-permute-done), channel_id=1, source_target_pairs={{0,1},{1,2},{2,3},{3,0},{4,5},{5,6},{6,7},{7,4},{8,9},{9,10},{10,1... | collective-permute-start | bytes 1966088 | tf_op jit(solution)/shard_map/ppermute | solution.py:24
  40.5 13.9 %collective-permute-start.2 = (bf16[1024,320]{0,1:T(8,128)(2,1)S(1)}, bf16[1024,320]{0,1:T(8,128)(2,1)S(1)}, u32[]{:S(2)}, u32[]{:S(2)}) collective-permute-start(bf16[1024,320]{0,1:T(8,128)(2,1)S(1)} %collective-permute-done.1), channel_id=1, source_target_pairs={{0,1},{1,2},{2,3},{3,0},{4,5},{5,6},{6,7},{7,4},{8,9},{9,10},{10,1... | collective-permute-start | bytes 1966088 | tf_op jit(solution)/shard_map/ppermute | solution.py:24
  55.8 2.4 copy-start
  115.1 6.2 %copy-start.5 = (f32[1280]{0:T(1024)S(1)}, f32[1280]{0:T(1024)}, u32[]{:S(2)}) copy-start(f32[1280]{0:T(1024)} %param.15) | copy-start | bytes 15364
  115.1 6.2 %copy-start.6 = (f32[1280]{0:T(1024)S(1)}, f32[1280]{0:T(1024)}, u32[]{:S(2)}) copy-start(f32[1280]{0:T(1024)} %param.13) | copy-start | bytes 15364
  115.1 6.2 %copy-start.7 = (f32[1280]{0:T(1024)S(1)}, f32[1280]{0:T(1024)}, u32[]{:S(2)}) copy-start(f32[1280]{0:T(1024)} %param.12) | copy-start | bytes 15364
  121.3 22.4 %copy-start.2 = (s32[16384]{0:T(1024)S(1)}, s32[16384]{0:T(1024)}, u32[]{:S(2)}) copy-start(s32[16384]{0:T(1024)} %param.21) | copy-start | bytes 196612
  143.6 33.2 %copy-start.3 = (f32[320]{0:T(512)S(1)}, f32[320]{0:T(512)}, u32[]{:S(2)}) copy-start(f32[320]{0:T(512)} %param.17) | copy-start | bytes 3844
  143.6 62.5 %reduce-scatter.7.cloned.1.call-start = ((), (), s32[]{:S(2)}) async-start(), calls=%async_computation.5 | async-start | bytes 819200
  178.2 29.1 %copy-start.8 = (f32[320]{0:T(512)S(1)}, f32[320]{0:T(512)}, u32[]{:S(2)}) copy-start(f32[320]{0:T(512)} %param.19) | copy-start | bytes 3844
  178.6 56.4 %copy-start.4 = (bf16[512,320]{0,1:T(8,128)(2,1)S(1)}, bf16[512,320]{0,1:T(8,128)(2,1)}, u32[]{:S(2)}) copy-start(bf16[512,320]{0,1:T(8,128)(2,1)} %param.20) | copy-start | bytes 983044
  208.5 26.5 %all-to-all-start = ((bf16[64,8,320]{2,1,0:T(8,128)(2,1)}), bf16[64,8,320]{2,1,0:T(8,128)(2,1)S(1)}, u32[]{:S(2)}, u32[]{:S(2)}) async-start(bf16[64,8,320]{2,1,0:T(8,128)(2,1)} %bitcast.9), calls=%async_computation.1 | async-start | bytes 786432 | tf_op jit(solution)/shard_map/all_to_all | solution.py:76
Sparse Core Ops, SparseCore 0:
  10.1 90.6 all-gather.3
  143.8 33.0 reduce-scatter.4
  183.2 22.8 reduce-scatter.6
